TPU v7x, 32 devices: a whole 2x2x4 slice. The times are simulated.
32 devices in a mesh: fsdp: 4 (over x, core), ctx: 2 (over y), tp: 4 (over z).
Axes of the slice: x: 2, y: 2, z: 4, core: 2. Of those that a mesh axis runs over, the one named last changes fastest.
Arguments:
- inputs: bfloat16 [2048, 8, 768], P('ctx', 'fsdp'), may hold values from -6 to 6
- thoughts: bfloat16 [6, 8, 768], P(None, 'fsdp'), may hold values from -6 to 6
- positions: int32 [6, 8], P(None, 'fsdp'), may hold values from 0 to 2047, as said below
- lengths: int32 [8, 3], P('fsdp'), may hold values from 1 to 1024, 2048 in all within a row
- w_qkv: bfloat16 [3, 768, 768], P(None, 'fsdp', 'tp'), may hold values from -0.21875 to 0.21875
- w_out: bfloat16 [768, 768], P('tp', 'fsdp'), may hold values from -3.5 to 3.5
- w_fc: bfloat16 [768, 3072], P('fsdp', 'tp'), may hold values from -0.21875 to 0.21875
- w_proj: bfloat16 [3072, 768], P('tp', 'fsdp'), may hold values from -0.109375 to 0.109375
- norm_gains: bfloat16 [2, 768], P(None, 'fsdp'), may hold values from 0.099609375 to 1.8984375
- norm_biases: bfloat16 [2, 768], P(None, 'fsdp'), may hold values from -0.14941406 to 0.14941406
- out_grad: bfloat16 [2048, 8, 768], P('ctx', 'fsdp'), may hold values from -6 to 6
Outputs:
- output: bfloat16 [2048, 8, 768], P('ctx', 'fsdp')
- d_inputs: float32 [2048, 8, 768], P('ctx', 'fsdp')
- d_thoughts: float32 [6, 8, 768], P(None, 'fsdp')
- d_w_qkv: float32 [3, 768, 768], P(None, 'fsdp', 'tp')
- d_w_out: float32 [768, 768], P('tp', 'fsdp')
- d_w_fc: float32 [768, 3072], P('fsdp', 'tp')
- d_w_proj: float32 [3072, 768], P('tp', 'fsdp')
- d_norm_gains: float32 [2, 768], P(None, 'fsdp')
- d_bias_first: float32 [768], P('fsdp')
- d_bias_second: float32 [768], P('fsdp')
Inputs may be any that keep to these rules, and one draw needn't show every extreme that they name: Each entry is a position of its sequence; the 6 positions of one sequence are distinct.
All inputs are finite; a program needn't handle non-finite values.
Results may differ from a plain program's by a relative error of at most 0.017.
Values may be sent and summed in bfloat16 or wider, within the bound.
A program may use at most 192 MiB of HBM per device.

v0:
```python
import jax
import jax.numpy as jnp
from jax import lax
from jax.sharding import PartitionSpec as P

HEAD_DIM = 64
EPSILON = 1e-05
NEGATIVE = -1000000000.0
PRECISE = lax.Precision.HIGHEST


def norm_rows(values, gain_row, offset):
    centre = jnp.mean(values, axis=-1, keepdims=True)
    shifted = values - centre
    spread = jnp.mean(shifted * shifted, axis=-1, keepdims=True)
    return shifted * lax.rsqrt(spread + EPSILON) * gain_row + offset


def gelu_tanh(values):
    return jax.nn.gelu(values, approximate=True)


def segment_ids(lengths, length):
    doc_ends = jnp.cumsum(lengths, axis=1, dtype=jnp.int32)
    places = jnp.arange(length, dtype=jnp.int32)
    return jnp.sum((places[:, None, None] >= doc_ends[None, :, :]).astype(jnp.int32), axis=2)


def seq_group(source, block_index, group_size):
    return lax.dynamic_slice_in_dim(source, block_index * group_size, group_size, 1)


def ungroup(stacked, row_count, seq_count):
    return jnp.moveaxis(stacked, 0, 1).reshape(row_count, seq_count, -1)


def heads_first(values):
    return jnp.moveaxis(values, 2, 0)


def heads_back(values):
    return jnp.moveaxis(values, 0, 2)


def score_head(query_head, key_head, query_pos, key_pos, query_seg, key_seg, score_scale):
    scores = (
        jnp.einsum("qgd,kgd->gqk", query_head, key_head, preferred_element_type=jnp.float32)
        * score_scale
    )
    causal = query_pos[:, None] >= key_pos[None, :]
    same_doc = query_seg.T[:, :, None] == key_seg.T[:, None, :]
    allowed = causal[None] & same_doc
    return (jnp.where(allowed, scores, NEGATIVE), allowed)


def head_back(
    query_head,
    key_head,
    value_head,
    grad_head,
    log_head,
    query_pos,
    key_pos,
    query_seg,
    key_seg,
    score_scale,
):
    scores, allowed = score_head(
        query_head, key_head, query_pos, key_pos, query_seg, key_seg, score_scale
    )
    attn_probs = jnp.where(allowed, jnp.exp(scores - log_head[..., None]), 0.0)
    d_probs = jnp.einsum("qgd,kgd->gqk", grad_head, value_head, preferred_element_type=jnp.float32)
    row_delta = jnp.sum(attn_probs * d_probs, axis=-1)
    d_scores = (attn_probs * (d_probs - row_delta[..., None])).astype(jnp.bfloat16)
    d_query = (
        jnp.einsum("gqk,kgd->qgd", d_scores, key_head, preferred_element_type=jnp.float32)
        * score_scale
    )
    d_keys = (
        jnp.einsum("gqk,qgd->kgd", d_scores, query_head, preferred_element_type=jnp.float32)
        * score_scale
    )
    d_values = jnp.einsum(
        "gqk,qgd->kgd",
        attn_probs.astype(jnp.bfloat16),
        grad_head,
        preferred_element_type=jnp.float32,
    )
    return (d_query, row_delta, d_keys, d_values)


def local(
    inputs,
    thoughts,
    positions,
    lengths,
    w_qkv,
    w_out,
    w_fc,
    w_proj,
    norm_gains,
    norm_biases,
    out_grad,
):
    row_count, seq_count, model_width = inputs.shape
    ctx_count = lax.axis_size("ctx")
    seq_length = row_count * ctx_count
    first_row = lax.axis_index("ctx") * row_count
    group_size = max(1, min(seq_count, 512 // row_count))
    block_count = seq_count // group_size
    token_count = row_count * seq_count
    score_scale = HEAD_DIM ** (-0.5)
    qkv_full, out_full, fc_full, proj_full, gain_rows, offset_rows = (
        lax.all_gather(w_qkv, "fsdp", axis=1, tiled=True),
        lax.all_gather(w_out, "fsdp", axis=1, tiled=True),
        lax.all_gather(w_fc, "fsdp", axis=0, tiled=True),
        lax.all_gather(w_proj, "fsdp", axis=1, tiled=True),
        lax.all_gather(norm_gains, "fsdp", axis=1, tiled=True),
        lax.all_gather(norm_biases, "fsdp", axis=1, tiled=True),
    )
    gain_rows = gain_rows.astype(jnp.float32)
    offset_rows = offset_rows.astype(jnp.float32)
    local_width = qkv_full.shape[2]
    local_heads = local_width // HEAD_DIM
    qkv_matrix = jnp.transpose(qkv_full, (1, 0, 2)).reshape(model_width, 3 * local_width)
    row_places = first_row + jnp.arange(row_count, dtype=jnp.int32)
    key_places = jnp.arange(seq_length, dtype=jnp.int32)
    select = (row_places[:, None, None] == positions[None, :, :]).astype(jnp.float32)
    keep_rows = 1.0 - jnp.sum(select, axis=1)
    start_rows = inputs.astype(jnp.float32) * keep_rows[:, :, None] + jnp.einsum(
        "rts,tsd->rsd", select, thoughts.astype(jnp.float32), precision=PRECISE
    )
    start_flat = start_rows.reshape(token_count, model_width)
    normed = norm_rows(start_flat, gain_rows[0], offset_rows[0]).astype(jnp.bfloat16)
    projected = jnp.dot(normed, qkv_matrix, preferred_element_type=jnp.float32)
    queries = (
        projected[:, :local_width]
        .astype(jnp.bfloat16)
        .reshape(row_count, seq_count, local_heads, HEAD_DIM)
    )
    keys_values = (
        projected[:, local_width:]
        .astype(jnp.bfloat16)
        .reshape(row_count, seq_count, 2 * local_width)
    )
    seg_all = segment_ids(lengths, seq_length)
    seg_rows = lax.dynamic_slice_in_dim(seg_all, first_row, row_count, 0)

    def split_pairs(whole_kv, count):
        key_part = whole_kv[..., :local_width].reshape(count, group_size, local_heads, HEAD_DIM)
        value_part = whole_kv[..., local_width:].reshape(count, group_size, local_heads, HEAD_DIM)
        return (key_part, value_part)

    def forward_block(block_index):
        whole_kv = lax.all_gather(
            seq_group(keys_values, block_index, group_size), "ctx", axis=0, tiled=True
        )
        key_part, value_part = split_pairs(whole_kv, seq_length)
        query_seg = seq_group(seg_rows, block_index, group_size)
        key_seg = seq_group(seg_all, block_index, group_size)

        def forward_one_head(triple):
            query_head, key_head, value_head = triple
            scores, allowed = score_head(
                query_head, key_head, row_places, key_places, query_seg, key_seg, score_scale
            )
            top_score = jnp.max(scores, axis=-1, keepdims=True)
            raised = jnp.exp(scores - top_score)
            row_total = jnp.sum(raised, axis=-1, keepdims=True)
            attn_probs = (raised / row_total).astype(jnp.bfloat16)
            mixed_rows = jnp.einsum(
                "gqk,kgd->qgd", attn_probs, value_head, preferred_element_type=jnp.float32
            )
            return (mixed_rows, (top_score + jnp.log(row_total))[..., 0])

        mixed_heads, log_heads = lax.map(
            forward_one_head,
            (
                heads_first(seq_group(queries, block_index, group_size)),
                heads_first(key_part),
                heads_first(value_part),
            ),
        )
        return (heads_back(mixed_heads), jnp.moveaxis(log_heads, 0, 1))

    attended, log_totals = lax.map(forward_block, jnp.arange(block_count))
    attended_b = (
        ungroup(attended, row_count, seq_count)
        .reshape(token_count, local_width)
        .astype(jnp.bfloat16)
    )
    attention = lax.psum(jnp.dot(attended_b, out_full, preferred_element_type=jnp.float32), "tp")
    middle = start_flat + attention
    normed_mid = norm_rows(middle, gain_rows[1], offset_rows[1]).astype(jnp.bfloat16)
    expanded = jnp.dot(normed_mid, fc_full, preferred_element_type=jnp.float32)
    activated = gelu_tanh(expanded).astype(jnp.bfloat16)
    feedforward = lax.psum(
        jnp.dot(activated, proj_full, preferred_element_type=jnp.float32).astype(jnp.bfloat16), "tp"
    ).astype(jnp.float32)
    output = (middle + feedforward).astype(jnp.bfloat16).reshape(row_count, seq_count, model_width)
    grad_rows = out_grad.reshape(token_count, model_width)
    d_proj = jnp.einsum("nf,nd->fd", activated, grad_rows, preferred_element_type=jnp.float32)
    d_activated = jnp.einsum("nd,fd->nf", grad_rows, proj_full, preferred_element_type=jnp.float32)
    gelu_back = jax.vjp(gelu_tanh, expanded)[1]
    d_expanded = gelu_back(d_activated)[0].astype(jnp.bfloat16)
    d_fc = jnp.einsum("nd,nf->df", normed_mid, d_expanded, preferred_element_type=jnp.float32)
    d_normed_mid = lax.psum(
        jnp.einsum("nf,df->nd", d_expanded, fc_full, preferred_element_type=jnp.float32), "tp"
    )
    mid_back = jax.vjp(norm_rows, middle, gain_rows[1], offset_rows[1])[1]
    d_middle, d_gain_mid, d_offset_mid = mid_back(d_normed_mid)
    d_middle = d_middle + grad_rows.astype(jnp.float32)
    d_attention = d_middle.astype(jnp.bfloat16)
    d_out = jnp.einsum("nc,nd->cd", attended_b, d_attention, preferred_element_type=jnp.float32)
    d_attended = jnp.einsum("nd,cd->nc", d_attention, out_full, preferred_element_type=jnp.float32)
    d_attended = d_attended.astype(jnp.bfloat16).reshape(
        row_count, seq_count, local_heads, HEAD_DIM
    )

    def fetch_keys(block_index):
        whole_kv = lax.all_gather(
            seq_group(keys_values, block_index, group_size), "ctx", axis=0, tiled=True
        )
        return split_pairs(whole_kv, seq_length)

    def query_side(block_index, log_block):
        key_part, value_part = fetch_keys(block_index)
        query_seg = seq_group(seg_rows, block_index, group_size)
        key_seg = seq_group(seg_all, block_index, group_size)

        def query_one_head(five):
            query_head, key_head, value_head, grad_head, log_head = five
            return head_back(
                query_head,
                key_head,
                value_head,
                grad_head,
                log_head,
                row_places,
                key_places,
                query_seg,
                key_seg,
                score_scale,
            )

        return lax.map(
            query_one_head,
            (
                heads_first(seq_group(queries, block_index, group_size)),
                heads_first(key_part),
                heads_first(value_part),
                heads_first(seq_group(d_attended, block_index, group_size)),
                jnp.moveaxis(log_block, 1, 0),
            ),
        )

    def backward_block(block_pair):
        block_index, log_block = block_pair
        d_query, row_delta, d_keys, d_values = query_side(block_index, log_block)
        term = jnp.concatenate(
            [
                heads_back(d_keys).reshape(seq_length, group_size, local_width),
                heads_back(d_values).reshape(seq_length, group_size, local_width),
            ],
            axis=-1,
        )
        return (
            heads_back(d_query),
            lax.psum_scatter(
                term.astype(jnp.bfloat16), "ctx", scatter_dimension=0, tiled=True
            ).astype(jnp.float32),
        )

    d_queries, d_kv = lax.map(backward_block, (jnp.arange(block_count), log_totals))
    d_query_rows = ungroup(d_queries, row_count, seq_count).reshape(token_count, local_width)
    d_kv_rows = ungroup(d_kv, row_count, seq_count).reshape(token_count, 2 * local_width)
    d_projected = jnp.concatenate([d_query_rows, d_kv_rows], axis=1).astype(jnp.bfloat16)
    d_qkv = jnp.einsum("nd,nc->dc", normed, d_projected, preferred_element_type=jnp.float32)
    d_qkv = jnp.transpose(d_qkv.reshape(model_width, 3, local_width), (1, 0, 2))
    d_normed = lax.psum(
        jnp.einsum("nc,dc->nd", d_projected, qkv_matrix, preferred_element_type=jnp.float32).astype(
            jnp.bfloat16
        ),
        "tp",
    ).astype(jnp.float32)
    first_back = jax.vjp(norm_rows, start_flat, gain_rows[0], offset_rows[0])[1]
    d_start, d_gain_first, d_offset_first = first_back(d_normed)
    d_start_rows = (d_start + d_middle).reshape(row_count, seq_count, model_width)
    d_inputs = d_start_rows * keep_rows[:, :, None]
    d_thoughts = jnp.einsum("rts,rsd->tsd", select, d_start_rows, precision=PRECISE)
    d_gains = jnp.stack([d_gain_first, d_gain_mid])
    d_offsets = jnp.stack([d_offset_first, d_offset_mid])
    shares = (
        lax.psum_scatter(
            d_qkv.astype(jnp.bfloat16), "fsdp", scatter_dimension=1, tiled=True
        ).astype(jnp.float32),
        lax.psum_scatter(
            d_out.astype(jnp.bfloat16), "fsdp", scatter_dimension=1, tiled=True
        ).astype(jnp.float32),
        lax.psum_scatter(d_fc.astype(jnp.bfloat16), "fsdp", scatter_dimension=0, tiled=True).astype(
            jnp.float32
        ),
        lax.psum_scatter(
            d_proj.astype(jnp.bfloat16), "fsdp", scatter_dimension=1, tiled=True
        ).astype(jnp.float32),
        lax.psum_scatter(
            d_gains.astype(jnp.bfloat16), "fsdp", scatter_dimension=1, tiled=True
        ).astype(jnp.float32),
        lax.psum_scatter(
            d_offsets.astype(jnp.bfloat16), "fsdp", scatter_dimension=1, tiled=True
        ).astype(jnp.float32),
    )
    summed = (
        lax.psum(shares[0].astype(jnp.bfloat16), "ctx").astype(jnp.float32),
        lax.psum(shares[1].astype(jnp.bfloat16), "ctx").astype(jnp.float32),
        lax.psum(shares[2].astype(jnp.bfloat16), "ctx").astype(jnp.float32),
        lax.psum(shares[3].astype(jnp.bfloat16), "ctx").astype(jnp.float32),
        lax.psum(shares[4].astype(jnp.bfloat16), "ctx").astype(jnp.float32),
        lax.psum(shares[5].astype(jnp.bfloat16), "ctx").astype(jnp.float32),
        lax.psum(d_thoughts.astype(jnp.bfloat16), "ctx").astype(jnp.float32),
    )
    return (
        output,
        d_inputs,
        summed[6],
        summed[0],
        summed[1],
        summed[2],
        summed[3],
        summed[4],
        summed[5][0],
        summed[5][1],
    )


def solution(mesh):
    in_specs = (
        P("ctx", "fsdp", None),
        P(None, "fsdp", None),
        P(None, "fsdp"),
        P("fsdp", None),
        P(None, "fsdp", "tp"),
        P("tp", "fsdp"),
        P("fsdp", "tp"),
        P("tp", "fsdp"),
        P(None, "fsdp"),
        P(None, "fsdp"),
        P("ctx", "fsdp", None),
    )
    out_specs = (
        P("ctx", "fsdp", None),
        P("ctx", "fsdp", None),
        P(None, "fsdp", None),
        P(None, "fsdp", "tp"),
        P("tp", "fsdp"),
        P("fsdp", "tp"),
        P("tp", "fsdp"),
        P(None, "fsdp"),
        P("fsdp"),
        P("fsdp"),
    )
    return jax.shard_map(local, mesh=mesh, in_specs=in_specs, out_specs=out_specs, check_vma=False)
```

profile of v0, /device:TPU:0, one launch (start us, length us, event | category | flops | bytes accessed | tf_op | source)
XLA Modules:
  0.0 1466.0 jit_solution(1052572031871166158)
XLA Ops:
  8.1 6.3 all-gather
  23.3 13.1 all_gather.26
  71.5 123.2 %while.55 = (s32[]{:T(128)}, bf16[2,1024,1,3,64]{1,4,3,2,0:T(8,128)(2,1)}, f32[2,1,3,1024]{3,0,2,1:T(2,128)S(1)}, s32[2]{0:T(128)S(1)}, bf16[1024,2,3,64]{0,3,1,...) while((s32[]{:T(128)}, ...), condition=%wide.region_10.11_spmd.clone, body=%wide.region_5.10_spmd.clone.sunk | while | flops 559939584 | bytes 42727944 | solution.py:186
  76.1 27.9 %all-gather.11.cloned.1.call-done = bf16[2048,1,384]{0,2,1:T(8,128)(2,1)} async-done(((bf16[1024,1,384]{0,2,1:T(8,128)(2,1)}), bf16[2048,1,384]{0,2,1:T(8,128)(2,1)}) %all-gather.11.cloned.1.call-update) | async-done | bytes 1572880 | tf_op jit(solution)/shard_map/while/body/eval_jaxpr/all_gather | solution.py:155
  106.4 25.7 %while.58 = (s32[]{:T(128)}, bf16[3,1024,1,64]{1,3,2,0:T(8,128)(2,1)}, f32[3,1,1024]{2,1,0:T(1,128)S(1)}, bf16[3,2048,1,64]{1,3,2,0:T(8,128)(2,1)}, s32[1024]{0:...) while((s32[]{:T(128)}, ...), condition=%wide.region_9.9_spmd, body=%wide.region_6.8_spmd.sunk | while | flops 559938560 | bytes 29296816 | solution.py:176
  138.3 26.5 %all-gather.11.cloned.1.call-done = bf16[2048,1,384]{0,2,1:T(8,128)(2,1)} async-done(((bf16[1024,1,384]{0,2,1:T(8,128)(2,1)}), bf16[2048,1,384]{0,2,1:T(8,128)(2,1)}) %all-gather.11.cloned.1.call-update) | async-done | bytes 1572880 | tf_op jit(solution)/shard_map/while/body/eval_jaxpr/all_gather | solution.py:155
  167.2 25.7 %while.58 = (s32[]{:T(128)}, bf16[3,1024,1,64]{1,3,2,0:T(8,128)(2,1)}, f32[3,1,1024]{2,1,0:T(1,128)S(1)}, bf16[3,2048,1,64]{1,3,2,0:T(8,128)(2,1)}, s32[1024]{0:...) while((s32[]{:T(128)}, ...), condition=%wide.region_9.9_spmd, body=%wide.region_6.8_spmd.sunk | while | flops 559938560 | bytes 29296816 | solution.py:176
  203.7 8.7 all_gather.27
  217.5 10.3 copy.142
  227.8 7.7 reshape.379
  235.5 8.5 reshape.374
  244.1 7.5 fusion.95
  251.5 188.5 %all-reduce.8.cloned.1.call-done = f32[2048,768]{1,0:T(8,128)} async-done(((f32[2048,768]{1,0:T(8,128)}), f32[2048,768]{1,0:T(8,128)}) %all-reduce.8.cloned.1.call-update) | async-done | bytes 6291472 | tf_op jit(solution)/shard_map/psum | solution.py:192
  450.2 10.0 fusion.62
  466.5 8.1 reshape.398
  474.6 213.9 %all-reduce.10.cloned.1.call-done = f32[2048,768]{1,0:T(8,128)} async-done(((f32[2048,768]{1,0:T(8,128)}), f32[2048,768]{1,0:T(8,128)}) %all-reduce.10.cloned.1.call-update) | async-done | bytes 6291472 | tf_op jit(solution)/shard_map/psum | solution.py:207
  688.5 6.4 multiply_reduce_fusion.1
  715.9 280.1 %while.57 = (s32[]{:T(128)}, bf16[2,1024,1,3,64]{1,4,3,2,0:T(8,128)(2,1)}, bf16[2,1024,1,384]{1,3,2,0:T(8,128)(2,1)}, s32[2]{0:T(128)S(1)}, bf16[1024,2,3,64]{0,...) while((s32[]{:T(128)}, ...), condition=%wide.region_23.24_spmd.clone, body=%wide.region_18.23_spmd.clone.sunk | while | flops 1373175808 | bytes 154253136 | solution.py:274
  721.0 25.1 %all-gather.13.cloned.1.call-done = bf16[2048,1,384]{0,2,1:T(8,128)(2,1)} async-done(((bf16[1024,1,384]{0,2,1:T(8,128)(2,1)}), bf16[2048,1,384]{0,2,1:T(8,128)(2,1)}) %all-gather.13.cloned.1.call-update) | async-done | bytes 1572880 | tf_op jit(solution)/shard_map/while/body/eval_jaxpr/all_gather | solution.py:221
  748.7 75.5 %while.59 = (s32[]{:T(128)}, bf16[3,1024,1,64]{1,3,2,0:T(8,128)(2,1)}, bf16[3,2048,1,64]{1,3,2,0:T(8,128)(2,1)}, bf16[3,2048,1,64]{1,3,2,0:T(8,128)(2,1)}, bf16[...) while((s32[]{:T(128)}, ...), condition=%wide.region_21.21_spmd, body=%wide.region_19.20_spmd.sunk | while | flops 1369635840 | bytes 108578080 | solution.py:246
  751.0 7.2 multiply_reduce_fusion.6
  758.2 6.6 multiply_convert_fusion.5
  776.2 7.2 multiply_reduce_fusion.6
  783.3 6.6 multiply_convert_fusion.5
  801.3 7.2 multiply_reduce_fusion.6
  808.5 6.6 multiply_convert_fusion.5
  828.9 24.5 %reduce-scatter.28.cloned.1.call-done = bf16[1024,1,384]{0,2,1:T(8,128)(2,1)} async-done(((bf16[2048,1,384]{0,2,1:T(8,128)(2,1)}), bf16[1024,1,384]{0,2,1:T(8,128)(2,1)}) %reduce-scatter.28.cloned.1.call-update) | async-done | bytes 786448 | tf_op jit(solution)/shard_map/while/body/eval_jaxpr/reduce_scatter | solution.py:269
  860.4 26.1 %all-gather.13.cloned.1.call-done = bf16[2048,1,384]{0,2,1:T(8,128)(2,1)} async-done(((bf16[1024,1,384]{0,2,1:T(8,128)(2,1)}), bf16[2048,1,384]{0,2,1:T(8,128)(2,1)}) %all-gather.13.cloned.1.call-update) | async-done | bytes 1572880 | tf_op jit(solution)/shard_map/while/body/eval_jaxpr/all_gather | solution.py:221
  889.2 75.5 %while.59 = (s32[]{:T(128)}, bf16[3,1024,1,64]{1,3,2,0:T(8,128)(2,1)}, bf16[3,2048,1,64]{1,3,2,0:T(8,128)(2,1)}, bf16[3,2048,1,64]{1,3,2,0:T(8,128)(2,1)}, bf16[...) while((s32[]{:T(128)}, ...), condition=%wide.region_21.21_spmd, body=%wide.region_19.20_spmd.sunk | while | flops 1369635840 | bytes 108578080 | solution.py:246
  891.5 7.2 multiply_reduce_fusion.6
  898.6 6.6 multiply_convert_fusion.5
  916.6 7.2 multiply_reduce_fusion.6
  923.8 6.6 multiply_convert_fusion.5
  941.8 7.2 multiply_reduce_fusion.6
  949.0 6.6 multiply_convert_fusion.5
  969.4 24.5 %reduce-scatter.28.cloned.1.call-done = bf16[1024,1,384]{0,2,1:T(8,128)(2,1)} async-done(((bf16[2048,1,384]{0,2,1:T(8,128)(2,1)}), bf16[1024,1,384]{0,2,1:T(8,128)(2,1)}) %reduce-scatter.28.cloned.1.call-update) | async-done | bytes 786448 | tf_op jit(solution)/shard_map/while/body/eval_jaxpr/reduce_scatter | solution.py:269
  1023.2 6.6 convolution_convert_fusion.5
  1029.9 7.2 convolution_convert_fusion.4
  1038.8 8.6 reduce-scatter.20.cloned.1.call-done
  1049.6 26.3 %reduce-scatter.16.cloned.1.call-done = bf16[192,768]{1,0:T(8,128)(2,1)} async-done(((bf16[768,768]{1,0:T(8,128)(2,1)}), bf16[192,768]{1,0:T(8,128)(2,1)}) %reduce-scatter.16.cloned.1.call-update) | async-done | bytes 294928 | tf_op jit(solution)/shard_map/reduce_scatter | solution.py:300
  1075.9 28.2 %reduce-scatter.18.cloned.1.call-done = bf16[768,192]{0,1:T(8,128)(2,1)} async-done(((bf16[768,768]{0,1:T(8,128)(2,1)}), bf16[768,192]{0,1:T(8,128)(2,1)}) %reduce-scatter.18.cloned.1.call-update) | async-done | bytes 294928 | tf_op jit(solution)/shard_map/reduce_scatter | solution.py:303
  1104.2 8.7 convolution_convert_fusion.1
  1118.9 24.6 %all-reduce.14.cloned.1.call-done = (bf16[3,192,192]{1,2,0:T(8,128)(2,1)}, bf16[192,192]{1,0:T(8,128)(2,1)}, bf16[192,768]{1,0:T(8,128)(2,1)}, bf16[768,192]{0,1:T(8,128)(2,1)}) async-done(((bf16[3,192,192]{1,2,0:T(8,128)(2,1)}, bf16[192,192]{1,0:T(8,128)(2,1)}, bf16[192,768]{1,0:T(8,128)(2,1)}, bf16[768,192]{0,1:T(8,128)(2,1)}), (bf16[3,192,192]{1,2,0:T(8,128)(2,1)}, bf16[192,192]{1,0:T(8,128)(2,1)}, ...) | async-done | bytes 884752 | tf_op jit(solution)/shard_map/psum | solution.py:314
  1150.6 218.4 %all-reduce.12.cloned.1.call-done = (bf16[2048,768]{1,0:T(8,128)(2,1)}, bf16[2048,768]{1,0:T(8,128)(2,1)}) async-done(((bf16[2048,768]{1,0:T(8,128)(2,1)}, bf16[2048,768]{1,0:T(8,128)(2,1)}), (bf16[2048,768]{1,0:T(8,128)(2,1)}, bf16[2048,768]{1,0:T(8,128)(2,1)})) %all-reduce.12.cloned.1.call-update) | async-done | bytes 6291472 | tf_op jit(solution)/shard_map/psum | solution.py:280
  1391.4 8.2 reshape.381
  1415.0 10.3 copy.166
  1426.3 21.0 %reduce-scatter.26.cloned.1.call-done = bf16[192,2]{1,0:T(8,128)(2,1)} async-done(((bf16[768,2]{1,0:T(8,128)(2,1)}), bf16[192,2]{1,0:T(8,128)(2,1)}) %reduce-scatter.26.cloned.1.call-update) | async-done | bytes 784
  1448.1 8.4 all-reduce.1
  (446 shorter events, 337.8 us)
Async XLA Ops:
  8.0 30.5 %copy-start = (bf16[6,2,768]{2,1,0:T(2,128)(2,1)S(1)}, bf16[6,2,768]{2,1,0:T(2,128)(2,1)}, u32[]{:S(2)}) copy-start(bf16[6,2,768]{2,1,0:T(2,128)(2,1)} %param.20) | copy-start | bytes 55300
  8.0 34.2 %copy-start.37 = (s32[1024]{0:T(1024)}, s32[1024]{0:T(1024)S(1)}, u32[]{:S(2)}) copy-start(s32[1024]{0:T(1024)S(1)} %iota_add_fusion.2) | copy-start | bytes 12292
  15.0 29.2 %copy-start.35 = (f32[768]{0:T(1024)}, f32[768]{0:T(1024)S(1)}, u32[]{:S(2)}) copy-start(f32[768]{0:T(1024)S(1)} %get-tuple-element.553) | copy-start | bytes 9220
  22.0 20.2 %copy-start.31 = (f32[1024,2]{0,1:T(2,128)}, f32[1024,2]{0,1:T(2,128)S(1)}, u32[]{:S(2)}) copy-start(f32[1024,2]{0,1:T(2,128)S(1)} %broadcast_subtract_fusion) | copy-start | bytes 24580
  71.5 123.9 %copy-start.39 = (bf16[192,192]{1,0:T(8,128)(2,1)S(1)}, bf16[192,192]{1,0:T(8,128)(2,1)}, u32[]{:S(2)}) copy-start(bf16[192,192]{1,0:T(8,128)(2,1)} %param.24) | copy-start | bytes 221188
  71.7 32.3 %all-gather.11.cloned.1.call-start = ((), (), s32[]{:S(2)}) async-start(), calls=%async_computation.19 | async-start | bytes 2359296 | tf_op jit(solution)/shard_map/while/body/eval_jaxpr/all_gather | solution.py:155
  134.0 30.9 %all-gather.11.cloned.1.call-start = ((), (), s32[]{:S(2)}) async-start(), calls=%async_computation.19 | async-start | bytes 2359296 | tf_op jit(solution)/shard_map/while/body/eval_jaxpr/all_gather | solution.py:155
  194.8 49.3 %all-gather.9.cloned.1.call-start = ((), (), s32[]{:S(2)}) async-start(), calls=%async_computation.9 | async-start | bytes 1474560 | tf_op jit(solution)/shard_map/all_gather | solution.py:117
  195.4 244.6 %all-reduce.8.cloned.1.call-start = ((), (), s32[]{:S(2)}) async-start(), calls=%async_computation.7 | async-start | bytes 12582912 | tf_op jit(solution)/shard_map/psum | solution.py:192
  216.9 233.3 %all-gather.7.cloned.1.call-start = ((), (), s32[]{:S(2)}) async-start(), calls=%async_computation.8 | async-start | bytes 1474560 | tf_op jit(solution)/shard_map/all_gather | solution.py:116
  217.5 471.0 %all-reduce.10.cloned.1.call-start = ((), (), s32[]{:S(2)}) async-start(), calls=%async_computation.10 | async-start | bytes 12582912 | tf_op jit(solution)/shard_map/psum | solution.py:207
  450.2 11.8 copy-start.49
  703.4 12.5 copy-start.30
  716.0 32.7 %copy-start.5 = (bf16[1024,2,384]{0,2,1:T(8,128)(2,1)}, bf16[1024,2,384]{0,2,1:T(8,128)(2,1)S(1)}, u32[]{:S(2)}) copy-start(bf16[1024,2,384]{0,2,1:T(8,128)(2,1)S(1)} %get-tuple-element.1164) | copy-start | bytes 4718596 | tf_op jit(solution)/shard_map/while
  716.0 32.7 %copy-start.13 = (bf16[1024,2,3,64]{0,3,1,2:T(8,128)(2,1)}, bf16[1024,2,3,64]{0,3,1,2:T(8,128)(2,1)S(1)}, u32[]{:S(2)}) copy-start(bf16[1024,2,3,64]{0,3,1,2:T(8,128)(2,1)S(1)} %get-tuple-element.1163) | copy-start | bytes 2359300 | tf_op jit(solution)/shard_map/while
  716.0 30.0 %all-gather.13.cloned.1.call-start = ((), (), s32[]{:S(2)}) async-start(), calls=%async_computation.20 | async-start | bytes 2359296 | tf_op jit(solution)/shard_map/while/body/eval_jaxpr/all_gather | solution.py:221
  719.7 133.6 %reduce-scatter.28.cloned.1.call-start = ((), (), s32[]{:S(2)}) async-start(), calls=%async_computation.21 | async-start | bytes 2359296 | tf_op jit(solution)/shard_map/while/body/eval_jaxpr/reduce_scatter | solution.py:269
  764.8 7.4 copy-start.16
  789.9 7.4 copy-start.16
  815.1 7.4 copy-start.16
  824.3 31.2 %copy-start.6 = (bf16[1024,2,384]{0,2,1:T(8,128)(2,1)S(1)}, bf16[1024,2,384]{0,2,1:T(8,128)(2,1)}, u32[]{:S(2)}) copy-start(bf16[1024,2,384]{0,2,1:T(8,128)(2,1)} %copy-done.5) | copy-start | bytes 4718596 | tf_op jit(solution)/shard_map/while
  824.3 31.2 %copy-start.14 = (bf16[1024,2,3,64]{0,3,1,2:T(8,128)(2,1)S(1)}, bf16[1024,2,3,64]{0,3,1,2:T(8,128)(2,1)}, u32[]{:S(2)}) copy-start(bf16[1024,2,3,64]{0,3,1,2:T(8,128)(2,1)} %copy-done.13) | copy-start | bytes 2359300 | tf_op jit(solution)/shard_map/while
  855.4 33.8 %copy-start.5 = (bf16[1024,2,384]{0,2,1:T(8,128)(2,1)}, bf16[1024,2,384]{0,2,1:T(8,128)(2,1)S(1)}, u32[]{:S(2)}) copy-start(bf16[1024,2,384]{0,2,1:T(8,128)(2,1)S(1)} %get-tuple-element.1164) | copy-start | bytes 4718596 | tf_op jit(solution)/shard_map/while
  855.4 33.8 %copy-start.13 = (bf16[1024,2,3,64]{0,3,1,2:T(8,128)(2,1)}, bf16[1024,2,3,64]{0,3,1,2:T(8,128)(2,1)S(1)}, u32[]{:S(2)}) copy-start(bf16[1024,2,3,64]{0,3,1,2:T(8,128)(2,1)S(1)} %get-tuple-element.1163) | copy-start | bytes 2359300 | tf_op jit(solution)/shard_map/while
  855.4 31.1 %all-gather.13.cloned.1.call-start = ((), (), s32[]{:S(2)}) async-start(), calls=%async_computation.20 | async-start | bytes 2359296 | tf_op jit(solution)/shard_map/while/body/eval_jaxpr/all_gather | solution.py:221
  859.1 134.7 %reduce-scatter.28.cloned.1.call-start = ((), (), s32[]{:S(2)}) async-start(), calls=%async_computation.21 | async-start | bytes 2359296 | tf_op jit(solution)/shard_map/while/body/eval_jaxpr/reduce_scatter | solution.py:269
  905.2 7.4 copy-start.16
  955.5 7.4 copy-start.16
  964.7 31.2 %copy-start.6 = (bf16[1024,2,384]{0,2,1:T(8,128)(2,1)S(1)}, bf16[1024,2,384]{0,2,1:T(8,128)(2,1)}, u32[]{:S(2)}) copy-start(bf16[1024,2,384]{0,2,1:T(8,128)(2,1)} %copy-done.5) | copy-start | bytes 4718596 | tf_op jit(solution)/shard_map/while
  964.7 31.2 %copy-start.14 = (bf16[1024,2,3,64]{0,3,1,2:T(8,128)(2,1)S(1)}, bf16[1024,2,3,64]{0,3,1,2:T(8,128)(2,1)}, u32[]{:S(2)}) copy-start(bf16[1024,2,3,64]{0,3,1,2:T(8,128)(2,1)} %copy-done.13) | copy-start | bytes 2359300 | tf_op jit(solution)/shard_map/while
  995.9 41.3 %reduce-scatter.22.cloned.1.call-start = ((), (), s32[]{:S(2)}) async-start(), calls=%async_computation.14 | async-start | bytes 491520
  996.5 51.0 %reduce-scatter.20.cloned.1.call-start = ((), (), s32[]{:S(2)}) async-start(), calls=%async_computation.13 | async-start | bytes 1228800
  1018.7 11.2 copy-start.10
  1023.0 52.9 %reduce-scatter.16.cloned.1.call-start = ((), (), s32[]{:S(2)}) async-start(), calls=%async_computation.11 | async-start | bytes 1474560 | tf_op jit(solution)/shard_map/reduce_scatter | solution.py:300
  1029.8 74.3 %reduce-scatter.18.cloned.1.call-start = ((), (), s32[]{:S(2)}) async-start(), calls=%async_computation.12 | async-start | bytes 1474560 | tf_op jit(solution)/shard_map/reduce_scatter | solution.py:303
  1037.1 106.3 %all-reduce.14.cloned.1.call-start = ((), (), s32[]{:S(2)}) async-start(), calls=%async_computation.18 | async-start | bytes 1966080 | tf_op jit(solution)/shard_map/psum | solution.py:314
  1104.2 8.8 copy-start.23
  1104.2 8.8 copy-start.24
  1104.2 8.8 copy-start.28
  1104.2 264.8 %all-reduce.12.cloned.1.call-start = ((), (), s32[]{:S(2)}) async-start(), calls=%async_computation.17 | async-start | bytes 12582912 | tf_op jit(solution)/shard_map/psum | solution.py:280
  1117.2 308.2 %reduce-scatter.24.cloned.1.call-start = ((), (), s32[]{:S(2)}) async-start(), calls=%async_computation.15 | async-start | bytes 245760
  1369.0 8.6 copy-start.36
  1377.6 9.2 slice-start.2
  1391.4 8.2 copy-start.32
  1399.6 7.9 copy-start.38
  1399.6 7.9 copy-start.44
  1406.4 40.9 %reduce-scatter.26.cloned.1.call-start = ((), (), s32[]{:S(2)}) async-start(), calls=%async_computation.16 | async-start | bytes 245760
  1412.3 46.0 %copy-start.1 = (bf16[6,2,768]{2,1,0:T(2,128)(2,1)S(1)}, bf16[6,2,768]{2,1,0:T(2,128)(2,1)}, u32[]{:S(2)}) copy-start(bf16[6,2,768]{2,1,0:T(2,128)(2,1)} %param.20) | copy-start | bytes 55300
  (64 other events, 202.9 us)
Sparse Core Ops, SparseCore 0:
  75.4 28.5 all-gather.10
  137.6 27.1 all-gather.10
  217.0 222.9 all-reduce.7
  466.7 221.7 all-reduce.9
  719.8 26.1 all-gather.12
  827.2 26.0 reduce-scatter.27
  859.3 27.1 all-gather.12
  967.7 26.0 reduce-scatter.27
  1104.3 39.1 all-reduce.13
  1145.7 223.2 all-reduce.11
Sparse Core Ops, SparseCore 1:
  196.8 19.4 all-gather.8
  218.9 17.4 all-gather.6
  999.5 20.7 reduce-scatter.21
  1023.0 24.4 reduce-scatter.19
  1050.3 25.6 reduce-scatter.15
  1078.5 25.6 reduce-scatter.17
  1406.4 18.7 reduce-scatter.23
  1427.5 19.7 reduce-scatter.25
where the time goes:
time: 1480 us; the launch traced here: 1470 us
  waiting for transfers between devices  886 us (60%)
  matrix products  218 us (15%)
  local copies, waits for them, and re-layouts  176 us (12%)
  other arithmetic  116 us (8%)
  blocking collectives  42.1 us (3%)
  between operations  16.5 us (1%)
    psum x1, waiting for transfers between devices, local(): lax.psum(jnp.einsum('nc,dc->nd', d_projected, qkv_matrix, preferred_eleme...  218 us
    psum x1, waiting for transfers between devices, local(): lax.psum(jnp.einsum('nf,df->nd', d_expanded, fc_full, preferred_element_t...  214 us
    psum x1, waiting for transfers between devices, local(): lax.psum(jnp.dot(attended_b, out_full, preferred_element_type=jnp.float32...  188 us
    dot_general x12, matrix products, score_head(): jnp.einsum('qgd,kgd->gqk', query_head, key_head, preferred_element_type=j...  62.1 us
    all_gather x2, waiting for transfers between devices, forward_block(): lax.all_gather(seq_group(keys_values, block_index, group_size), 'ctx', ax...  54.4 us
    all_gather x2, waiting for transfers between devices, fetch_keys(): lax.all_gather(seq_group(keys_values, block_index, group_size), 'ctx', ax...  51.2 us
    reduce_scatter x2, waiting for transfers between devices, backward_block(): lax.psum_scatter(term.astype(jnp.bfloat16), 'ctx', scatter_dimension=0, t...  48.9 us
    unnamed x106, local copies, waits for them, and re-layouts  48.5 us
  transfers between devices with their start and end apart: 18, of which 14 were waited for; matrix products, arithmetic and copies ran while one was open for 11% of the time, Pallas kernels for 0%

commit v1 on v0

--- a/solution.py
+++ b/solution.py
@@ -7,6 +7,25 @@
 EPSILON = 1e-05
 NEGATIVE = -1000000000.0
 PRECISE = lax.Precision.HIGHEST
+
+
+def joined_along(blocks, dim):
+    blocks = jnp.moveaxis(blocks, 0, dim)
+    shape = blocks.shape
+    return blocks.reshape(*shape[:dim], shape[dim] * shape[dim + 1], *shape[dim + 2 :])
+
+
+def doubled(x, axis):
+    size, index = (lax.axis_size(axis), lax.axis_index(axis))
+    blocks, bit = (x[None], 1)
+    while bit < size:
+        partner_block = lax.ppermute(blocks, axis, [(i, i ^ bit) for i in range(size)])
+        low = index & bit == 0
+        blocks = jnp.concatenate(
+            [jnp.where(low, blocks, partner_block), jnp.where(low, partner_block, blocks)]
+        )
+        bit *= 2
+    return blocks
 
 
 def norm_rows(values, gain_row, offset):
@@ -152,9 +171,8 @@
         return (key_part, value_part)
 
     def forward_block(block_index):
-        whole_kv = lax.all_gather(
-            seq_group(keys_values, block_index, group_size), "ctx", axis=0, tiled=True
-        )
+        x = seq_group(keys_values, block_index, group_size)
+        whole_kv = joined_along(doubled(x, "ctx"), 0)
         key_part, value_part = split_pairs(whole_kv, seq_length)
         query_seg = seq_group(seg_rows, block_index, group_size)
         key_seg = seq_group(seg_all, block_index, group_size)

time: 1480 us -> 1460 us (0.986)
  waiting for transfers between devices: 886 us -> 866 us
    all_gather x2 -> x0, waiting for transfers between devices: 54.4 us -> none  [forward_block(): lax.all_gather(seq_group(keys_values, block_index, group_size), 'ctx', ax...]
    ppermute x0 -> x2, waiting for transfers between devices: none -> 36.3 us  [doubled(): lax.ppermute(blocks, axis, [(i, i ^ bit) for i in range(size)])]
    unnamed x106 -> x109, local copies, waits for them, and re-layouts: 48.5 us -> 48 us
  transfers between devices with their start and end apart: 18 -> 18, of which waited for: 14 -> 14; matrix products, arithmetic and copies ran while one was open for 11% -> 17% of each run, Pallas kernels for 0% -> 0%
where the time goes in v1:
time: 1460 us; the launch traced here: 1450 us
  waiting for transfers between devices  866 us (59%)
  matrix products  217 us (15%)
  local copies, waits for them, and re-layouts  175 us (12%)
  other arithmetic  120 us (8%)
  blocking collectives  40.8 us (3%)
  between operations  16.8 us (1%)
    psum x1, waiting for transfers between devices, local(): lax.psum(jnp.einsum('nc,dc->nd', d_projected, qkv_matrix, preferred_eleme...  219 us
    psum x1, waiting for transfers between devices, local(): lax.psum(jnp.einsum('nf,df->nd', d_expanded, fc_full, preferred_element_t...  209 us
    psum x1, waiting for transfers between devices, local(): lax.psum(jnp.dot(attended_b, out_full, preferred_element_type=jnp.float32...  190 us
    dot_general x12, matrix products, score_head(): jnp.einsum('qgd,kgd->gqk', query_head, key_head, preferred_element_type=j...  62.5 us
    all_gather x2, waiting for transfers between devices, fetch_keys(): lax.all_gather(seq_group(keys_values, block_index, group_size), 'ctx', ax...  51.2 us
    reduce_scatter x2, waiting for transfers between devices, backward_block(): lax.psum_scatter(term.astype(jnp.bfloat16), 'ctx', scatter_dimension=0, t...  48.9 us
    unnamed x109, local copies, waits for them, and re-layouts  48 us
    convert_element_type x6, other arithmetic, head_back(): (attn_probs * (d_probs - row_delta[..., None])).astype(jnp.bfloat16)  39.3 us
  transfers between devices with their start and end apart: 18, of which 14 were waited for; matrix products, arithmetic and copies ran while one was open for 17% of the time, Pallas kernels for 0%

profile of v1, /device:TPU:0, one launch (start us, length us, event | category | flops | bytes accessed | tf_op | source)
XLA Modules:
  0.0 1447.8 jit_solution(6269633003471216985)
XLA Ops:
  8.8 6.3 all-gather
  24.0 14.5 all_gather.23
  69.9 111.5 %while.55 = (s32[]{:T(128)}, bf16[2,1024,1,3,64]{1,4,3,2,0:T(8,128)(2,1)}, f32[2,1,3,1024]{3,0,2,1:T(2,128)S(1)}, s32[2]{0:T(128)S(1)}, bf16[1024,2,3,64]{0,3,1,...) while((s32[]{:T(128)}, ...), condition=%wide.region_10.11_spmd.clone, body=%wide.region_5.10_spmd.clone.sunk | while | flops 561512448 | bytes 60816008 | solution.py:204
  75.3 18.5 %collective-permute-done = bf16[1,1024,1,384]{3,1,2,0:T(8,128)(2,1)} collective-permute-done((bf16[1,1024,1,384]{3,1,2,0:T(8,128)(2,1)}, bf16[1,1024,1,384]{3,1,2,0:T(8,128)(2,1)}, u32[]{:S(2)}, u32[]{:S(2)}) %collective-permute-start) | collective-permute-done | bytes 786464 | tf_op jit(solution)/shard_map/while/body/eval_jaxpr/ppermute | solution.py:22
  98.4 25.9 %while.58 = (s32[]{:T(128)}, bf16[3,1024,1,64]{1,3,2,0:T(8,128)(2,1)}, f32[3,1,1024]{2,1,0:T(1,128)S(1)}, bf16[3,2048,1,64]{1,3,2,0:T(8,128)(2,1)}, s32[1024]{0:...) while((s32[]{:T(128)}, ...), condition=%wide.region_9.9_spmd, body=%wide.region_6.8_spmd.sunk | while | flops 559938560 | bytes 29296816 | solution.py:194
  131.3 17.7 %collective-permute-done = bf16[1,1024,1,384]{3,1,2,0:T(8,128)(2,1)} collective-permute-done((bf16[1,1024,1,384]{3,1,2,0:T(8,128)(2,1)}, bf16[1,1024,1,384]{3,1,2,0:T(8,128)(2,1)}, u32[]{:S(2)}, u32[]{:S(2)}) %collective-permute-start) | collective-permute-done | bytes 786464 | tf_op jit(solution)/shard_map/while/body/eval_jaxpr/ppermute | solution.py:22
  153.6 25.9 %while.58 = (s32[]{:T(128)}, bf16[3,1024,1,64]{1,3,2,0:T(8,128)(2,1)}, f32[3,1,1024]{2,1,0:T(1,128)S(1)}, bf16[3,2048,1,64]{1,3,2,0:T(8,128)(2,1)}, s32[1024]{0:...) while((s32[]{:T(128)}, ...), condition=%wide.region_9.9_spmd, body=%wide.region_6.8_spmd.sunk | while | flops 559938560 | bytes 29296816 | solution.py:194
  186.9 6.1 all_gather.24
  199.5 10.3 copy.150
  209.8 6.8 reshape.382
  216.6 9.3 reshape.377
  231.7 190.0 %all-reduce.8.cloned.1.call-done = f32[2048,768]{1,0:T(8,128)} async-done(((f32[2048,768]{1,0:T(8,128)}), f32[2048,768]{1,0:T(8,128)}) %all-reduce.8.cloned.1.call-update) | async-done | bytes 6291472 | tf_op jit(solution)/shard_map/psum | solution.py:210
  432.0 10.1 fusion.62
  448.4 7.6 reshape.402
  461.0 209.1 %all-reduce.10.cloned.1.call-done = f32[2048,768]{1,0:T(8,128)} async-done(((f32[2048,768]{1,0:T(8,128)}), f32[2048,768]{1,0:T(8,128)}) %all-reduce.10.cloned.1.call-update) | async-done | bytes 6291472 | tf_op jit(solution)/shard_map/psum | solution.py:225
  670.1 6.6 multiply_reduce_fusion.1
  694.3 281.7 %while.57 = (s32[]{:T(128)}, bf16[2,1024,1,3,64]{1,4,3,2,0:T(8,128)(2,1)}, bf16[2,1024,1,384]{1,3,2,0:T(8,128)(2,1)}, s32[2]{0:T(128)S(1)}, bf16[1024,2,3,64]{0,...) while((s32[]{:T(128)}, ...), condition=%wide.region_23.24_spmd.clone, body=%wide.region_18.23_spmd.clone.sunk | while | flops 1373175808 | bytes 141670160 | solution.py:292
  700.2 25.1 %all-gather.10.cloned.1.call-done = bf16[2048,1,384]{0,2,1:T(8,128)(2,1)} async-done(((bf16[1024,1,384]{0,2,1:T(8,128)(2,1)}), bf16[2048,1,384]{0,2,1:T(8,128)(2,1)}) %all-gather.10.cloned.1.call-update) | async-done | bytes 1572880 | tf_op jit(solution)/shard_map/while/body/eval_jaxpr/all_gather | solution.py:239
  728.0 75.5 %while.59 = (s32[]{:T(128)}, bf16[3,1024,1,64]{1,3,2,0:T(8,128)(2,1)}, bf16[3,2048,1,64]{1,3,2,0:T(8,128)(2,1)}, bf16[3,2048,1,64]{1,3,2,0:T(8,128)(2,1)}, bf16[...) while((s32[]{:T(128)}, ...), condition=%wide.region_21.21_spmd, body=%wide.region_19.20_spmd.sunk | while | flops 1369635840 | bytes 108578080 | solution.py:264
  730.3 7.2 multiply_reduce_fusion.6
  737.4 6.6 multiply_convert_fusion.5
  755.4 7.2 multiply_reduce_fusion.6
  762.6 6.6 multiply_convert_fusion.5
  780.6 7.2 multiply_reduce_fusion.6
  787.8 6.6 multiply_convert_fusion.5
  808.1 24.4 %reduce-scatter.28.cloned.1.call-done = bf16[1024,1,384]{0,2,1:T(8,128)(2,1)} async-done(((bf16[2048,1,384]{0,2,1:T(8,128)(2,1)}), bf16[1024,1,384]{0,2,1:T(8,128)(2,1)}) %reduce-scatter.28.cloned.1.call-update) | async-done | bytes 786448 | tf_op jit(solution)/shard_map/while/body/eval_jaxpr/reduce_scatter | solution.py:287
  840.6 26.1 %all-gather.10.cloned.1.call-done = bf16[2048,1,384]{0,2,1:T(8,128)(2,1)} async-done(((bf16[1024,1,384]{0,2,1:T(8,128)(2,1)}), bf16[2048,1,384]{0,2,1:T(8,128)(2,1)}) %all-gather.10.cloned.1.call-update) | async-done | bytes 1572880 | tf_op jit(solution)/shard_map/while/body/eval_jaxpr/all_gather | solution.py:239
  869.4 75.5 %while.59 = (s32[]{:T(128)}, bf16[3,1024,1,64]{1,3,2,0:T(8,128)(2,1)}, bf16[3,2048,1,64]{1,3,2,0:T(8,128)(2,1)}, bf16[3,2048,1,64]{1,3,2,0:T(8,128)(2,1)}, bf16[...) while((s32[]{:T(128)}, ...), condition=%wide.region_21.21_spmd, body=%wide.region_19.20_spmd.sunk | while | flops 1369635840 | bytes 108578080 | solution.py:264
  871.7 7.2 multiply_reduce_fusion.6
  878.8 6.6 multiply_convert_fusion.5
  896.8 7.2 multiply_reduce_fusion.6
  904.0 6.6 multiply_convert_fusion.5
  922.0 7.2 multiply_reduce_fusion.6
  929.1 6.6 multiply_convert_fusion.5
  949.5 24.5 %reduce-scatter.28.cloned.1.call-done = bf16[1024,1,384]{0,2,1:T(8,128)(2,1)} async-done(((bf16[2048,1,384]{0,2,1:T(8,128)(2,1)}), bf16[1024,1,384]{0,2,1:T(8,128)(2,1)}) %reduce-scatter.28.cloned.1.call-update) | async-done | bytes 786448 | tf_op jit(solution)/shard_map/while/body/eval_jaxpr/reduce_scatter | solution.py:287
  1003.7 6.6 convolution_convert_fusion.5
  1010.3 7.2 convolution_convert_fusion.4
  1019.5 8.8 reduce-scatter.20.cloned.1.call-done
  1030.4 26.4 %reduce-scatter.16.cloned.1.call-done = bf16[192,768]{1,0:T(8,128)(2,1)} async-done(((bf16[768,768]{1,0:T(8,128)(2,1)}), bf16[192,768]{1,0:T(8,128)(2,1)}) %reduce-scatter.16.cloned.1.call-update) | async-done | bytes 294928 | tf_op jit(solution)/shard_map/reduce_scatter | solution.py:318
  1056.8 28.7 %reduce-scatter.18.cloned.1.call-done = bf16[768,192]{0,1:T(8,128)(2,1)} async-done(((bf16[768,768]{0,1:T(8,128)(2,1)}), bf16[768,192]{0,1:T(8,128)(2,1)}) %reduce-scatter.18.cloned.1.call-update) | async-done | bytes 294928 | tf_op jit(solution)/shard_map/reduce_scatter | solution.py:321
  1085.6 8.8 convolution_convert_fusion.1
  1100.3 24.2 %all-reduce.14.cloned.1.call-done = (bf16[3,192,192]{1,2,0:T(8,128)(2,1)}, bf16[192,192]{1,0:T(8,128)(2,1)}, bf16[192,768]{1,0:T(8,128)(2,1)}, bf16[768,192]{0,1:T(8,128)(2,1)}) async-done(((bf16[3,192,192]{1,2,0:T(8,128)(2,1)}, bf16[192,192]{1,0:T(8,128)(2,1)}, bf16[192,768]{1,0:T(8,128)(2,1)}, bf16[768,192]{0,1:T(8,128)(2,1)}), (bf16[3,192,192]{1,2,0:T(8,128)(2,1)}, bf16[192,192]{1,0:T(8,128)(2,1)}, ...) | async-done | bytes 884752 | tf_op jit(solution)/shard_map/psum | solution.py:332
  1131.7 218.9 %all-reduce.12.cloned.1.call-done = (bf16[2048,768]{1,0:T(8,128)(2,1)}, bf16[2048,768]{1,0:T(8,128)(2,1)}) async-done(((bf16[2048,768]{1,0:T(8,128)(2,1)}, bf16[2048,768]{1,0:T(8,128)(2,1)}), (bf16[2048,768]{1,0:T(8,128)(2,1)}, bf16[2048,768]{1,0:T(8,128)(2,1)})) %all-reduce.12.cloned.1.call-update) | async-done | bytes 6291472 | tf_op jit(solution)/shard_map/psum | solution.py:298
  1350.6 6.1 add_convert_fusion
  1373.0 8.2 reshape.384
  1396.7 10.3 copy.174
  1407.9 21.0 %reduce-scatter.26.cloned.1.call-done = bf16[192,2]{1,0:T(8,128)(2,1)} async-done(((bf16[768,2]{1,0:T(8,128)(2,1)}), bf16[192,2]{1,0:T(8,128)(2,1)}) %reduce-scatter.26.cloned.1.call-update) | async-done | bytes 784
  1429.7 8.4 all-reduce.1
  (455 shorter events, 343.2 us)
Async XLA Ops:
  8.0 32.5 %copy-start = (bf16[6,2,768]{2,1,0:T(2,128)(2,1)S(1)}, bf16[6,2,768]{2,1,0:T(2,128)(2,1)}, u32[]{:S(2)}) copy-start(bf16[6,2,768]{2,1,0:T(2,128)(2,1)} %param.20) | copy-start | bytes 55300
  8.0 217.9 %all-gather.8.cloned.1.call-start = ((), (), s32[]{:S(2)}) async-start(), calls=%async_computation.9 | async-start | bytes 1474560 | tf_op jit(solution)/shard_map/all_gather | solution.py:136
  8.8 413.0 %all-reduce.8.cloned.1.call-start = ((), (), s32[]{:S(2)}) async-start(), calls=%async_computation.7 | async-start | bytes 12582912 | tf_op jit(solution)/shard_map/psum | solution.py:210
  8.8 35.5 %copy-start.38 = (s32[1024]{0:T(1024)}, s32[1024]{0:T(1024)S(1)}, u32[]{:S(2)}) copy-start(s32[1024]{0:T(1024)S(1)} %iota_add_fusion.2) | copy-start | bytes 12292
  15.8 30.6 %copy-start.36 = (f32[768]{0:T(1024)}, f32[768]{0:T(1024)S(1)}, u32[]{:S(2)}) copy-start(f32[768]{0:T(1024)S(1)} %get-tuple-element.553) | copy-start | bytes 9220
  22.8 21.5 %copy-start.32 = (f32[1024,2]{0,1:T(2,128)}, f32[1024,2]{0,1:T(2,128)S(1)}, u32[]{:S(2)}) copy-start(f32[1024,2]{0,1:T(2,128)S(1)} %broadcast_subtract_fusion) | copy-start | bytes 24580
  51.4 7.4 copy-start.12
  69.9 117.0 %copy-start.31 = (bf16[192,192]{0,1:T(8,128)(2,1)S(1)}, bf16[192,192]{0,1:T(8,128)(2,1)}, u32[]{:S(2)}) copy-start(bf16[192,192]{0,1:T(8,128)(2,1)} %copy.162) | copy-start | bytes 221188
  70.1 25.3 %copy-start.5 = (bf16[1024,2,384]{2,0,1:T(8,128)(2,1)}, bf16[1024,2,384]{2,0,1:T(8,128)(2,1)S(1)}, u32[]{:S(2)}) copy-start(bf16[1024,2,384]{2,0,1:T(8,128)(2,1)S(1)} %get-tuple-element.1131) | copy-start | bytes 4718596 | tf_op jit(solution)/shard_map/while
  73.7 20.1 %collective-permute-start = (bf16[1,1024,1,384]{3,1,2,0:T(8,128)(2,1)}, bf16[1,1024,1,384]{3,1,2,0:T(8,128)(2,1)}, u32[]{:S(2)}, u32[]{:S(2)}) collective-permute-start(bf16[1,1024,1,384]{3,1,2,0:T(8,128)(2,1)} %dynamic-slice_bitcast_fusion.9), channel_id=1, source_target_pairs={{0,4},{4,0},{1,5},{5,1},{2,6},{6,2},{3,7},{7,3},{8,12},{12,8},{9,1... | collective-permute-start | bytes 2359304 | tf_op jit(solution)/shard_map/while/body/eval_jaxpr/ppermute | solution.py:22
  98.4 27.7 %copy-start.6 = (bf16[1024,2,384]{2,0,1:T(8,128)(2,1)S(1)}, bf16[1024,2,384]{2,0,1:T(8,128)(2,1)}, u32[]{:S(2)}) copy-start(bf16[1024,2,384]{2,0,1:T(8,128)(2,1)} %copy-done.5) | copy-start | bytes 4718596 | tf_op jit(solution)/shard_map/while
  126.1 24.4 %copy-start.5 = (bf16[1024,2,384]{2,0,1:T(8,128)(2,1)}, bf16[1024,2,384]{2,0,1:T(8,128)(2,1)S(1)}, u32[]{:S(2)}) copy-start(bf16[1024,2,384]{2,0,1:T(8,128)(2,1)S(1)} %get-tuple-element.1131) | copy-start | bytes 4718596 | tf_op jit(solution)/shard_map/while
  129.7 19.3 %collective-permute-start = (bf16[1,1024,1,384]{3,1,2,0:T(8,128)(2,1)}, bf16[1,1024,1,384]{3,1,2,0:T(8,128)(2,1)}, u32[]{:S(2)}, u32[]{:S(2)}) collective-permute-start(bf16[1,1024,1,384]{3,1,2,0:T(8,128)(2,1)} %dynamic-slice_bitcast_fusion.9), channel_id=1, source_target_pairs={{0,4},{4,0},{1,5},{5,1},{2,6},{6,2},{3,7},{7,3},{8,12},{12,8},{9,1... | collective-permute-start | bytes 2359304 | tf_op jit(solution)/shard_map/while/body/eval_jaxpr/ppermute | solution.py:22
  153.6 27.8 %copy-start.6 = (bf16[1024,2,384]{2,0,1:T(8,128)(2,1)S(1)}, bf16[1024,2,384]{2,0,1:T(8,128)(2,1)}, u32[]{:S(2)}) copy-start(bf16[1024,2,384]{2,0,1:T(8,128)(2,1)} %copy-done.5) | copy-start | bytes 4718596 | tf_op jit(solution)/shard_map/while
  181.4 17.3 %copy-start.13 = (bf16[1024,2,3,64]{0,3,1,2:T(8,128)(2,1)}, bf16[1024,2,3,64]{0,3,1,2:T(8,128)(2,1)S(1)}, u32[]{:S(2)}) copy-start(bf16[1024,2,3,64]{0,3,1,2:T(8,128)(2,1)S(1)} %get-tuple-element.1219) | copy-start | bytes 2359300
  198.7 233.3 %all-gather.6.cloned.1.call-start = ((), (), s32[]{:S(2)}) async-start(), calls=%async_computation.8 | async-start | bytes 1474560 | tf_op jit(solution)/shard_map/all_gather | solution.py:135
  199.5 470.7 %all-reduce.10.cloned.1.call-start = ((), (), s32[]{:S(2)}) async-start(), calls=%async_computation.10 | async-start | bytes 12582912 | tf_op jit(solution)/shard_map/psum | solution.py:225
  216.6 464.3 %copy-start.9 = (bf16[2048,768]{1,0:T(8,128)(2,1)}, bf16[2048,768]{1,0:T(8,128)(2,1)S(1)}, u32[]{:S(2)}) copy-start(bf16[2048,768]{1,0:T(8,128)(2,1)S(1)} %reshape.382) | copy-start | bytes 9437188
  432.0 11.9 copy-start.50
  694.3 33.7 %copy-start.22 = (bf16[1024,2,3,64]{0,3,1,2:T(8,128)(2,1)}, bf16[1024,2,3,64]{0,3,1,2:T(8,128)(2,1)S(1)}, u32[]{:S(2)}) copy-start(bf16[1024,2,3,64]{0,3,1,2:T(8,128)(2,1)S(1)} %get-tuple-element.1177) | copy-start | bytes 2359300 | tf_op jit(solution)/shard_map/while
  694.3 31.0 %all-gather.10.cloned.1.call-start = ((), (), s32[]{:S(2)}) async-start(), calls=%async_computation.19 | async-start | bytes 2359296 | tf_op jit(solution)/shard_map/while/body/eval_jaxpr/all_gather | solution.py:239
  699.0 133.6 %reduce-scatter.28.cloned.1.call-start = ((), (), s32[]{:S(2)}) async-start(), calls=%async_computation.20 | async-start | bytes 2359296 | tf_op jit(solution)/shard_map/while/body/eval_jaxpr/reduce_scatter | solution.py:287
  794.3 7.4 copy-start.15
  803.5 31.1 %copy-start.23 = (bf16[1024,2,3,64]{0,3,1,2:T(8,128)(2,1)S(1)}, bf16[1024,2,3,64]{0,3,1,2:T(8,128)(2,1)}, u32[]{:S(2)}) copy-start(bf16[1024,2,3,64]{0,3,1,2:T(8,128)(2,1)} %copy-done.22) | copy-start | bytes 2359300 | tf_op jit(solution)/shard_map/while
  834.6 34.8 %copy-start.22 = (bf16[1024,2,3,64]{0,3,1,2:T(8,128)(2,1)}, bf16[1024,2,3,64]{0,3,1,2:T(8,128)(2,1)S(1)}, u32[]{:S(2)}) copy-start(bf16[1024,2,3,64]{0,3,1,2:T(8,128)(2,1)S(1)} %get-tuple-element.1177) | copy-start | bytes 2359300 | tf_op jit(solution)/shard_map/while
  834.6 32.1 %all-gather.10.cloned.1.call-start = ((), (), s32[]{:S(2)}) async-start(), calls=%async_computation.19 | async-start | bytes 2359296 | tf_op jit(solution)/shard_map/while/body/eval_jaxpr/all_gather | solution.py:239
  839.3 134.6 %reduce-scatter.28.cloned.1.call-start = ((), (), s32[]{:S(2)}) async-start(), calls=%async_computation.20 | async-start | bytes 2359296 | tf_op jit(solution)/shard_map/while/body/eval_jaxpr/reduce_scatter | solution.py:287
  910.6 7.4 copy-start.15
  935.7 7.4 copy-start.15
  944.9 31.1 %copy-start.23 = (bf16[1024,2,3,64]{0,3,1,2:T(8,128)(2,1)S(1)}, bf16[1024,2,3,64]{0,3,1,2:T(8,128)(2,1)}, u32[]{:S(2)}) copy-start(bf16[1024,2,3,64]{0,3,1,2:T(8,128)(2,1)} %copy-done.22) | copy-start | bytes 2359300 | tf_op jit(solution)/shard_map/while
  976.0 41.8 %reduce-scatter.22.cloned.1.call-start = ((), (), s32[]{:S(2)}) async-start(), calls=%async_computation.14 | async-start | bytes 491520
  976.8 51.5 %reduce-scatter.20.cloned.1.call-start = ((), (), s32[]{:S(2)}) async-start(), calls=%async_computation.13 | async-start | bytes 1228800
  999.3 11.0 copy-start.10
  1003.6 53.1 %reduce-scatter.16.cloned.1.call-start = ((), (), s32[]{:S(2)}) async-start(), calls=%async_computation.11 | async-start | bytes 1474560 | tf_op jit(solution)/shard_map/reduce_scatter | solution.py:318
  1010.3 75.2 %reduce-scatter.18.cloned.1.call-start = ((), (), s32[]{:S(2)}) async-start(), calls=%async_computation.12 | async-start | bytes 1474560 | tf_op jit(solution)/shard_map/reduce_scatter | solution.py:321
  1017.6 107.0 %all-reduce.14.cloned.1.call-start = ((), (), s32[]{:S(2)}) async-start(), calls=%async_computation.18 | async-start | bytes 1966080 | tf_op jit(solution)/shard_map/psum | solution.py:332
  1085.5 8.9 copy-start.25
  1085.5 8.9 copy-start.26
  1085.5 8.9 copy-start.30
  1085.5 265.0 %all-reduce.12.cloned.1.call-start = ((), (), s32[]{:S(2)}) async-start(), calls=%async_computation.17 | async-start | bytes 12582912 | tf_op jit(solution)/shard_map/psum | solution.py:298
  1098.6 308.4 %reduce-scatter.24.cloned.1.call-start = ((), (), s32[]{:S(2)}) async-start(), calls=%async_computation.15 | async-start | bytes 245760
  1350.6 8.7 copy-start.37
  1359.2 9.2 slice-start.2
  1373.0 8.2 copy-start.33
  1381.2 8.0 copy-start.39
  1381.2 8.0 copy-start.45
  1388.0 40.9 %reduce-scatter.26.cloned.1.call-start = ((), (), s32[]{:S(2)}) async-start(), calls=%async_computation.16 | async-start | bytes 245760
  1394.0 45.9 %copy-start.1 = (bf16[6,2,768]{2,1,0:T(2,128)(2,1)S(1)}, bf16[6,2,768]{2,1,0:T(2,128)(2,1)}, u32[]{:S(2)}) copy-start(bf16[6,2,768]{2,1,0:T(2,128)(2,1)} %param.20) | copy-start | bytes 55300
  (65 other events, 213.8 us)
Sparse Core Ops, SparseCore 0:
  10.4 21.5 all-gather.7
  201.1 17.7 all-gather.5
  699.1 26.1 all-gather.9
  806.4 26.0 reduce-scatter.27
  839.5 27.1 all-gather.9
  947.8 26.0 reduce-scatter.27
  979.9 20.8 reduce-scatter.21
  1003.8 24.4 reduce-scatter.19
  1031.0 25.6 reduce-scatter.15
  1059.8 25.6 reduce-scatter.17
  1388.1 18.6 reduce-scatter.23
  1409.1 19.7 reduce-scatter.25
Sparse Core Ops, SparseCore 1:
  198.8 222.9 all-reduce.7
  448.5 221.5 all-reduce.9
  1085.6 38.9 all-reduce.13
  1127.5 223.0 all-reduce.11
